TPU v7x, 1024 devices: a whole 4x8x16 slice. The times are simulated.
1024 devices in a mesh: wide: 64 (over y, z_hi, x), narrow: 16 (over z_lo, core).
Axes of the slice: x: 4, y: 8, z: 16 (z_hi: 2, z_lo: 8; z = z_hi * 8 + z_lo), core: 2. Of those that a mesh axis runs over, the one named last changes fastest.
Arguments:
- state: float32 [2, 67108864], P(None, ('wide', 'narrow')), may hold values from -6 to 6
- gates: float32 [6, 2, 256, 256], replicated
- gate_bits: int32 [6, 8], replicated, may hold values from 7 to 15, as said below
- slot_plan: int32 [10], replicated, may hold values from 7 to 15, as said below
Outputs:
- final_state: float32 [2, 67108864], P(None, ('wide', 'narrow'))
Inputs may be any that keep to these rules, and one draw needn't show every extreme that they name: `gate_bits`: each gate's row names 8 different positions. `slot_plan`: the first 4 entries differ from one another, and so do the last 6.
All inputs are finite; a program needn't handle non-finite values.
Results may differ from a plain program's by a relative error of at most 0.0001.
Values sent between devices are 32-bit elements; how exact they have to be, the bound alone decides.
No kernel may reach another device: no remote copies, remote signals or barrier semaphores. Data moves between devices by JAX's collectives and lax.ppermute only.
A program may use at most 32 MiB of HBM per device.

v0:
```python
import functools

import jax
import jax.numpy as jnp
from jax import lax
from jax.experimental import pallas as pl
from jax.experimental.pallas import tpu as pltpu
from jax.sharding import PartitionSpec as P

LANE_BITS = 7
LANES = 2**LANE_BITS
ROW_BITS = 9
ROWS = 2**ROW_BITS
DIM_BITS = 8
DIM = 2**DIM_BITS

BF16 = jnp.bfloat16
F32 = jnp.float32


def mm(a, b):
    return jnp.dot(a, b, preferred_element_type=F32)


def split(x):
    high = x.astype(BF16)
    low = (x - high.astype(F32)).astype(BF16)
    return high, low


def gate_slots(bits, gate):
    used = [bits[gate, j] - LANE_BITS for j in range(DIM_BITS)]
    free = ROW_BITS * (ROW_BITS - 1) // 2 - sum(used)
    return used + [free]


def plan_slots(plan, start, count, rest):
    slots = [plan[start + b] - LANE_BITS for b in range(count)]
    filled = jnp.int32(0)
    for p in range(ROW_BITS):
        rest[filled] = jnp.int32(p)
        taken = functools.reduce(jnp.logical_or, [s == p for s in slots])
        filled = filled + jnp.where(taken, 0, 1).astype(jnp.int32)
    return [rest[k] for k in range(ROW_BITS - count)] + slots


def permutation(source, target, where):
    for place in range(ROW_BITS):
        where[target[place]] = jnp.int32(place)
    lane = lax.broadcasted_iota(jnp.int32, (8, ROWS), 1)
    moved = jnp.zeros((8, ROWS), jnp.int32)
    for place in range(ROW_BITS):
        moved = moved | (((lane >> place) & 1) << where[source[place]])
    row = lax.broadcasted_iota(jnp.int32, (ROWS, ROWS), 0)
    hit = jnp.broadcast_to(moved[:1], (ROWS, ROWS)) == row
    return jnp.where(hit, 1.0, 0.0).astype(BF16)


def stack_gate(real, imag):
    real_high, real_low = split(real)
    imag_high, imag_low = split(imag)
    return jnp.concatenate([real_high, imag_high, real_low, imag_low], axis=0)


def pack_parts(real, imag):
    real_high, real_low = split(real)
    imag_high, imag_low = split(imag)
    return jnp.concatenate([real_high, imag_high, real_low, imag_low], axis=1)


def complex_product(stack, high, low, width):
    half = stack.shape[0] // 2
    quarter = half // 2
    first = mm(stack, high)
    total = first[:half] + first[half:] + mm(stack[:half], low)
    real = total[:quarter, :width] - total[quarter:, width:]
    imag = total[:quarter, width:] + total[quarter:, :width]
    return real, imag


def gate_on_parts(stack, parts, width):
    reals, imags = [], []
    for free in range(2):
        rows = parts[free * DIM : (free + 1) * DIM]
        real, imag = complex_product(stack, rows[:, : 2 * width], rows[:, 2 * width :], width)
        reals.append(real)
        imags.append(imag)
    return jnp.concatenate(reals, axis=0), jnp.concatenate(imags, axis=0)


def first_kernel(narrow_bits, bits, plan, x, gates, out, where, rest):
    natural = list(range(ROW_BITS))
    order_a = gate_slots(bits, 0)
    order_b = gate_slots(bits, 1)
    order_out = plan_slots(plan, 0, narrow_bits, rest)
    parts = pack_parts(x[pl.ds(0, ROWS, stride=2), :], x[pl.ds(1, ROWS, stride=2), :])
    parts = mm(permutation(natural, order_a, where), parts).astype(BF16)
    real, imag = gate_on_parts(stack_gate(gates[0, 0], gates[0, 1]), parts, LANES)
    parts = pack_parts(real, imag)
    parts = mm(permutation(order_a, order_b, where), parts).astype(BF16)
    real, imag = gate_on_parts(stack_gate(gates[1, 0], gates[1, 1]), parts, LANES)
    parts = mm(permutation(order_b, order_out, where), pack_parts(real, imag))
    blocks = out.shape[0]
    shape = (blocks, ROWS // blocks, LANES)
    out[:, 0] = (parts[:, :LANES] + parts[:, 2 * LANES : 3 * LANES]).reshape(shape)
    out[:, 1] = (parts[:, LANES : 2 * LANES] + parts[:, 3 * LANES :]).reshape(shape)


def operator_kernel(section, order_in, order_out, bits, plan, gates, out, where, rest):
    order_a = gate_slots(bits, 2 * section)
    order_b = gate_slots(bits, 2 * section + 1)
    columns = order_in(plan, rest)
    result = order_out(plan, rest)
    pick = permutation(columns, order_a, where)
    stack = stack_gate(gates[0, 0], gates[0, 1])
    picked = [mm(stack, pick[free * DIM : (free + 1) * DIM]).astype(BF16) for free in range(2)]
    parts = jnp.concatenate(
        [
            jnp.concatenate([p[k * DIM : (k + 1) * DIM] for p in picked], axis=0)
            for k in range(4)
        ],
        axis=1,
    )
    parts = mm(permutation(order_a, order_b, where), parts).astype(BF16)
    real, imag = gate_on_parts(stack_gate(gates[1, 0], gates[1, 1]), parts, ROWS)
    final = permutation(order_b, result, where)
    for k, part in enumerate([*split(real), *split(imag)]):
        place = (k % 2) * 2 + k // 2
        out[place * ROWS : (place + 1) * ROWS, :] = mm(final, part).astype(BF16)


def apply_section(stack, x):
    real = x[:, 0].reshape(ROWS, LANES)
    imag = x[:, 1].reshape(ROWS, LANES)
    real_high, real_low = split(real)
    imag_high, imag_low = split(imag)
    high = jnp.concatenate([real_high, imag_high], axis=1)
    low = jnp.concatenate([real_low, imag_low], axis=1)
    return complex_product(stack, high, low, LANES)


def middle_kernel(stack, x, out):
    real, imag = apply_section(stack[...], x[...])
    blocks = out.shape[0]
    shape = (blocks, ROWS // blocks, LANES)
    out[:, 0] = real.reshape(shape)
    out[:, 1] = imag.reshape(shape)


def last_kernel(stack, x, out):
    real, imag = apply_section(stack[...], x[...])
    out[pl.ds(0, ROWS, stride=2), :] = real
    out[pl.ds(1, ROWS, stride=2), :] = imag


SMEM = pl.BlockSpec(memory_space=pltpu.SMEM)
VMEM = pl.BlockSpec(memory_space=pltpu.VMEM)
SCALARS = [pltpu.SMEM((ROW_BITS,), jnp.int32), pltpu.SMEM((ROW_BITS + 1,), jnp.int32)]
UNIT = 2 * DIM**3


def gates_spec(section):
    return pl.BlockSpec((2, 2, DIM, DIM), lambda i: (section, 0, 0, 0))


def cost(units, moved):
    return pl.CostEstimate(flops=units * UNIT, bytes_accessed=moved, transcendentals=0)


def first_section(x, gates, bits, plan, narrow_bits):
    blocks = 2**narrow_bits
    shape = (blocks, 2, ROWS // blocks, LANES)
    return pl.pallas_call(
        functools.partial(first_kernel, narrow_bits),
        grid=(1,),
        out_shape=jax.ShapeDtypeStruct(shape, F32),
        in_specs=[SMEM, SMEM, VMEM, gates_spec(0)],
        out_specs=VMEM,
        scratch_shapes=SCALARS,
        cost_estimate=cost(48, 2 * 2**20),
        name="first_section",
    )(bits, plan, x, gates)


def section_operator(section, gates, bits, plan, order_in, order_out):
    return pl.pallas_call(
        functools.partial(operator_kernel, section, order_in, order_out),
        grid=(1,),
        out_shape=jax.ShapeDtypeStruct((4 * ROWS, ROWS), BF16),
        in_specs=[SMEM, SMEM, gates_spec(section)],
        out_specs=VMEM,
        scratch_shapes=SCALARS,
        cost_estimate=cost(128, 3 * 2**20),
        name="section_operator",
    )(bits, plan, gates)


def run_section(kernel, stack, x, shape, name):
    return pl.pallas_call(
        kernel,
        out_shape=jax.ShapeDtypeStruct(shape, F32),
        in_specs=[VMEM, VMEM],
        out_specs=VMEM,
        cost_estimate=cost(24, 3 * 2**20),
        name=name,
    )(stack, x)


def exchange(blocks, axis):
    flat = blocks.reshape(blocks.shape[0], -1, LANES)
    flat = lax.all_to_all(flat, axis, split_axis=0, concat_axis=0, tiled=True)
    return flat.reshape(blocks.shape)


def shards(state, gates, gate_bits, slot_plan):
    narrow_bits = lax.axis_size("narrow").bit_length() - 1
    wide_bits = lax.axis_size("wide").bit_length() - 1
    x = state.reshape(2, ROWS, LANES).transpose(1, 0, 2).reshape(2 * ROWS, LANES)

    def narrow_order(plan, rest):
        return plan_slots(plan, 0, narrow_bits, rest)

    def wide_order(plan, rest):
        return plan_slots(plan, narrow_bits, wide_bits, rest)

    def natural(plan, rest):
        return list(range(ROW_BITS))

    blocks = first_section(x, gates, gate_bits, slot_plan, narrow_bits)
    second = section_operator(1, gates, gate_bits, slot_plan, narrow_order, wide_order)
    third = section_operator(2, gates, gate_bits, slot_plan, wide_order, natural)
    blocks = exchange(blocks, "narrow")
    wide = 2**wide_bits
    blocks = run_section(
        middle_kernel, second, blocks, (wide, 2, ROWS // wide, LANES), "middle_section"
    )
    blocks = exchange(blocks, "wide")
    x = run_section(last_kernel, third, blocks, (2 * ROWS, LANES), "last_section")
    return x.reshape(ROWS, 2, LANES).transpose(1, 0, 2).reshape(2, ROWS * LANES)


def solution(mesh):
    return jax.shard_map(
        shards,
        mesh=mesh,
        in_specs=(P(None, ("wide", "narrow")), P(), P(), P()),
        out_specs=P(None, ("wide", "narrow")),
        check_vma=False,
    )
```

profile of v0, /device:TPU:65, one launch (start us, length us, event | category | flops | bytes accessed | tf_op | source)
XLA Modules:
  0.0 114.3 jit_solution(1915672587569997480)
XLA Ops:
  0.0 4.8 %first_section.1 = f32[16,2,32,128]{3,2,1,0:T(8,128)} custom-call(s32[6,8]{1,0:T(8,128)} %bits.5, s32[10]{0:T(128)} %plan.5, f32[1024,128]{1,0:T(8,128)} %bitcast.18, f32[6,2,256,256]{3,2,1,0:T(8,128)} %gates.5), custom_call_target="tpu_custom_call" | custom-call | flops 1610612736 | bytes 2097152 | tf_op jit(solution)/shard_map/first_section/pallas_call | solution.py:173
  4.8 15.9 %all-to-all-start = ((f32[16,64,128]{2,1,0:T(8,128)}), f32[16,64,128]{2,1,0:T(8,128)S(1)}, u32[]{:S(2)}, u32[]{:S(2)}) async-start(f32[16,64,128]{2,1,0:T(8,128)} %bitcast.17), calls=%async_computation | async-start | bytes 1048576 | tf_op jit(solution)/shard_map/all_to_all | solution.py:211
  20.7 7.3 %section_operator.3.stack = bf16[2048,512]{1,0:T(8,128)(2,1)} custom-call(s32[6,8]{1,0:T(8,128)} %bits.5, s32[10]{0:T(128)} %plan.5, f32[6,2,256,256]{3,2,1,0:T(8,128)} %gates.5), custom_call_target="tpu_custom_call" | custom-call | flops 4294967296 | bytes 3145728 | tf_op jit(solution)/shard_map/section_operator/pallas_call | solution.py:186
  28.0 19.5 %all-to-all-done = f32[16,64,128]{2,1,0:T(8,128)S(1)} async-done(((f32[16,64,128]{2,1,0:T(8,128)}), f32[16,64,128]{2,1,0:T(8,128)S(1)}, u32[]{:S(2)}, u32[]{:S(2)}) %all-to-all-start) | async-done | bytes 524320 | tf_op jit(solution)/shard_map/all_to_all | solution.py:211
  47.5 0.0 copy-start
  47.5 0.8 copy-done
  48.3 3.5 %middle_section.1 = f32[64,2,8,128]{3,2,1,0:T(8,128)} custom-call(bf16[2048,512]{1,0:T(8,128)(2,1)} %section_operator.3.stack, f32[16,2,32,128]{3,2,1,0:T(8,128)} %bitcast.14), custom_call_target="tpu_custom_call" | custom-call | flops 805306368 | bytes 3145728 | tf_op jit(solution)/shard_map/middle_section/pallas_call | solution.py:199
  51.7 19.6 %all-to-all-start.1 = ((f32[64,16,128]{2,1,0:T(8,128)}), f32[64,16,128]{2,1,0:T(8,128)S(1)}, u32[]{:S(2)}, u32[]{:S(2)}) async-start(f32[64,16,128]{2,1,0:T(8,128)} %bitcast.16), calls=%async_computation.1 | async-start | bytes 1048576 | tf_op jit(solution)/shard_map/all_to_all | solution.py:211
  71.3 7.2 %section_operator.2.stack = bf16[2048,512]{1,0:T(8,128)(2,1)} custom-call(s32[6,8]{1,0:T(8,128)} %bits.5, s32[10]{0:T(128)} %plan.5, f32[6,2,256,256]{3,2,1,0:T(8,128)} %gates.5), custom_call_target="tpu_custom_call" | custom-call | flops 4294967296 | bytes 3145728 | tf_op jit(solution)/shard_map/section_operator/pallas_call | solution.py:186
  78.5 31.5 %all-to-all-done.1 = f32[64,16,128]{2,1,0:T(8,128)S(1)} async-done(((f32[64,16,128]{2,1,0:T(8,128)}), f32[64,16,128]{2,1,0:T(8,128)S(1)}, u32[]{:S(2)}, u32[]{:S(2)}) %all-to-all-start.1) | async-done | bytes 524320 | tf_op jit(solution)/shard_map/all_to_all | solution.py:211
  110.1 0.0 copy-start.1
  110.1 0.8 copy-done.1
  110.9 3.5 %last_section.1 = f32[1024,128]{1,0:T(8,128)} custom-call(bf16[2048,512]{1,0:T(8,128)(2,1)} %section_operator.2.stack, f32[64,2,8,128]{3,2,1,0:T(8,128)} %bitcast.15), custom_call_target="tpu_custom_call" | custom-call | flops 805306368 | bytes 3145728 | tf_op jit(solution)/shard_map/last_section/pallas_call | solution.py:199
Async XLA Ops:
  4.8 42.7 %all-to-all-start = ((f32[16,64,128]{2,1,0:T(8,128)}), f32[16,64,128]{2,1,0:T(8,128)S(1)}, u32[]{:S(2)}, u32[]{:S(2)}) async-start(f32[16,64,128]{2,1,0:T(8,128)} %bitcast.17), calls=%async_computation | async-start | bytes 1048576 | tf_op jit(solution)/shard_map/all_to_all | solution.py:211
  47.5 0.8 copy-start
  51.7 58.3 %all-to-all-start.1 = ((f32[64,16,128]{2,1,0:T(8,128)}), f32[64,16,128]{2,1,0:T(8,128)S(1)}, u32[]{:S(2)}, u32[]{:S(2)}) async-start(f32[64,16,128]{2,1,0:T(8,128)} %bitcast.16), calls=%async_computation.1 | async-start | bytes 1048576 | tf_op jit(solution)/shard_map/all_to_all | solution.py:211
  110.1 0.8 copy-start.1
where the time goes:
time: 115 us; the launch traced here: 114 us
  waiting for transfers between devices  51.1 us (44%)
  starting transfers between devices  35.5 us (31%)
  Pallas kernels  26.2 us (23%)
  local copies, waits for them, and re-layouts  1.58 us (1%)
    all_to_all x2, waiting for transfers between devices, exchange(): flat = lax.all_to_all(flat, axis, split_axis=0, concat_axis=0, tiled=True)  51.1 us
    all_to_all x2, starting transfers between devices, exchange(): flat = lax.all_to_all(flat, axis, split_axis=0, concat_axis=0, tiled=True)  35.5 us
    pallas_call x2, Pallas kernels, section_operator(): pl.pallas_call(functools.partial(operator_kernel, section, order_in, orde...  14.5 us
    pallas_call x2, Pallas kernels, run_section(): pl.pallas_call(kernel, out_shape=jax.ShapeDtypeStruct(shape, F32), in_spe...  6.91 us
    pallas_call x1, Pallas kernels, first_section(): pl.pallas_call(functools.partial(first_kernel, narrow_bits), grid=(1,), o...  4.76 us
  transfers between devices with their start and end apart: 2, of which 2 were waited for; matrix products, arithmetic and copies ran while one was open for 0% of the time, Pallas kernels for 13%

commit v1 on v0

--- a/solution.py
+++ b/solution.py
@@ -88,16 +88,25 @@
     return jnp.concatenate(reals, axis=0), jnp.concatenate(imags, axis=0)
 
 
-def first_kernel(narrow_bits, bits, plan, x, gates, out, where, rest):
+def first_kernel(narrow_bits, bits, plan, x_hbm, gates_hbm, out, where, rest, x, gates, sems):
+    copies = [pltpu.make_async_copy(x_hbm, x, sems.at[0])]
+    for gate in range(2):
+        copies.append(
+            pltpu.make_async_copy(gates_hbm.at[gate], gates.at[gate], sems.at[gate + 1])
+        )
+    for copy in copies:
+        copy.start()
     natural = list(range(ROW_BITS))
     order_a = gate_slots(bits, 0)
     order_b = gate_slots(bits, 1)
     order_out = plan_slots(plan, 0, narrow_bits, rest)
+    enter = permutation(natural, order_a, where)
+    for copy in copies:
+        copy.wait()
     parts = pack_parts(x[pl.ds(0, ROWS, stride=2), :], x[pl.ds(1, ROWS, stride=2), :])
-    parts = mm(permutation(natural, order_a, where), parts).astype(BF16)
+    parts = mm(enter, parts).astype(BF16)
     real, imag = gate_on_parts(stack_gate(gates[0, 0], gates[0, 1]), parts, LANES)
-    parts = pack_parts(real, imag)
-    parts = mm(permutation(order_a, order_b, where), parts).astype(BF16)
+    parts = mm(permutation(order_a, order_b, where), pack_parts(real, imag)).astype(BF16)
     real, imag = gate_on_parts(stack_gate(gates[1, 0], gates[1, 1]), parts, LANES)
     parts = mm(permutation(order_b, order_out, where), pack_parts(real, imag))
     blocks = out.shape[0]
@@ -155,6 +164,7 @@
 
 SMEM = pl.BlockSpec(memory_space=pltpu.SMEM)
 VMEM = pl.BlockSpec(memory_space=pltpu.VMEM)
+ANY = pl.BlockSpec(memory_space=pl.ANY)
 SCALARS = [pltpu.SMEM((ROW_BITS,), jnp.int32), pltpu.SMEM((ROW_BITS + 1,), jnp.int32)]
 UNIT = 2 * DIM**3
 
@@ -172,11 +182,15 @@
     shape = (blocks, 2, ROWS // blocks, LANES)
     return pl.pallas_call(
         functools.partial(first_kernel, narrow_bits),
-        grid=(1,),
-        out_shape=jax.ShapeDtypeStruct(shape, F32),
-        in_specs=[SMEM, SMEM, VMEM, gates_spec(0)],
+        out_shape=vmem_shape(shape, F32),
+        in_specs=[SMEM, SMEM, ANY, ANY],
         out_specs=VMEM,
-        scratch_shapes=SCALARS,
+        scratch_shapes=[
+            *SCALARS,
+            pltpu.VMEM(x.shape, F32),
+            pltpu.VMEM((2, *gates.shape[1:]), F32),
+            pltpu.SemaphoreType.DMA((3,)),
+        ],
         cost_estimate=cost(48, 2 * 2**20),
         name="first_section",
     )(bits, plan, x, gates)
@@ -186,7 +200,7 @@
     return pl.pallas_call(
         functools.partial(operator_kernel, section, order_in, order_out),
         grid=(1,),
-        out_shape=jax.ShapeDtypeStruct((4 * ROWS, ROWS), BF16),
+        out_shape=vmem_shape((4 * ROWS, ROWS), BF16),
         in_specs=[SMEM, SMEM, gates_spec(section)],
         out_specs=VMEM,
         scratch_shapes=SCALARS,
@@ -195,15 +209,23 @@
     )(bits, plan, gates)
 
 
-def run_section(kernel, stack, x, shape, name):
+def vmem_shape(shape, dtype):
+    return pltpu.VMEM(shape, dtype)
+
+
+def in_vmem(x):
+    return pltpu.with_memory_space_constraint(x, pltpu.VMEM)
+
+
+def run_section(kernel, stack, x, out_shape, name):
     return pl.pallas_call(
         kernel,
-        out_shape=jax.ShapeDtypeStruct(shape, F32),
+        out_shape=out_shape,
         in_specs=[VMEM, VMEM],
         out_specs=VMEM,
         cost_estimate=cost(24, 3 * 2**20),
         name=name,
-    )(stack, x)
+    )(in_vmem(stack), in_vmem(x))
 
 
 def exchange(blocks, axis):
@@ -231,11 +253,11 @@
     third = section_operator(2, gates, gate_bits, slot_plan, wide_order, natural)
     blocks = exchange(blocks, "narrow")
     wide = 2**wide_bits
-    blocks = run_section(
-        middle_kernel, second, blocks, (wide, 2, ROWS // wide, LANES), "middle_section"
-    )
+    shape = vmem_shape((wide, 2, ROWS // wide, LANES), F32)
+    blocks = run_section(middle_kernel, second, blocks, shape, "middle_section")
     blocks = exchange(blocks, "wide")
-    x = run_section(last_kernel, third, blocks, (2 * ROWS, LANES), "last_section")
+    shape = jax.ShapeDtypeStruct((2 * ROWS, LANES), F32)
+    x = run_section(last_kernel, third, blocks, shape, "last_section")
     return x.reshape(ROWS, 2, LANES).transpose(1, 0, 2).reshape(2, ROWS * LANES)
 
 

time: 115 us -> 111 us (0.965)
  Pallas kernels: 26.2 us -> 20.8 us
  waiting for transfers between devices: 51.1 us -> 53.7 us
  local copies, waits for them, and re-layouts: 1.58 us -> 0 us
    pallas_call x2, Pallas kernels: 14.5 us -> 11.8 us  [section_operator(): pl.pallas_call(functools.partial(operator_kernel, section, order_in, orde...]
    all_to_all x2, waiting for transfers between devices: 51.1 us -> 53.7 us  [exchange(): flat = lax.all_to_all(flat, axis, split_axis=0, concat_axis=0, tiled=True)]
    pallas_call x3, Pallas kernels: 11.7 us -> 9.04 us  [the longest x1 5.47 us: first_section(): pl.pallas_call(functools.partial(first_kernel, narrow_bits), out_shape=vm...]
    unnamed x4 -> x0, local copies, waits for them, and re-layouts: 1.58 us -> none
  transfers between devices with their start and end apart: 2 -> 2, of which waited for: 2 -> 2; matrix products, arithmetic and copies ran while one was open for 0% -> 0% of each run, Pallas kernels for 13% -> 11%
where the time goes in v1:
time: 111 us; the launch traced here: 110 us
  waiting for transfers between devices  53.7 us (48%)
  starting transfers between devices  35.5 us (32%)
  Pallas kernels  20.8 us (19%)
    all_to_all x2, waiting for transfers between devices, exchange(): flat = lax.all_to_all(flat, axis, split_axis=0, concat_axis=0, tiled=True)  53.7 us
    all_to_all x2, starting transfers between devices, exchange(): flat = lax.all_to_all(flat, axis, split_axis=0, concat_axis=0, tiled=True)  35.5 us
    pallas_call x2, Pallas kernels, section_operator(): pl.pallas_call(functools.partial(operator_kernel, section, order_in, orde...  11.8 us
    pallas_call x1, Pallas kernels, first_section(): pl.pallas_call(functools.partial(first_kernel, narrow_bits), out_shape=vm...  5.47 us
    pallas_call x2, Pallas kernels, run_section(): pl.pallas_call(kernel, out_shape=out_shape, in_specs=[VMEM, VMEM], out_sp...  3.57 us
  transfers between devices with their start and end apart: 2, of which 2 were waited for; matrix products, arithmetic and copies ran while one was open for 0% of the time, Pallas kernels for 11%

profile of v1, /device:TPU:65, one launch (start us, length us, event | category | flops | bytes accessed | tf_op | source)
XLA Modules:
  0.0 110.1 jit_solution(7020477741049833330)
XLA Ops:
  0.0 5.5 %first_section.1 = f32[16,2,32,128]{3,2,1,0:T(8,128)} custom-call(s32[6,8]{1,0:T(8,128)} %bits.5, s32[10]{0:T(128)} %plan.5, f32[1024,128]{1,0:T(8,128)} %bitcast.16, f32[6,2,256,256]{3,2,1,0:T(8,128)} %gates_hbm.1), custom_call_target="tpu_custom_call" | custom-call | flops 1610612736 | bytes 2097152 | tf_op jit(solution)/shard_map/first_section/pallas_call | solution.py:183
  5.5 15.9 %all-to-all-start = ((f32[16,64,128]{2,1,0:T(8,128)}), f32[16,64,128]{2,1,0:T(8,128)S(1)}, u32[]{:S(2)}, u32[]{:S(2)}) async-start(f32[16,64,128]{2,1,0:T(8,128)} %bitcast.3), calls=%async_computation | async-start | bytes 1048576 | tf_op jit(solution)/shard_map/all_to_all | solution.py:233
  21.4 5.9 %section_operator.3.stack = bf16[2048,512]{1,0:T(8,128)(2,1)S(1)} custom-call(s32[6,8]{1,0:T(8,128)} %bits.5, s32[10]{0:T(128)} %plan.5, f32[6,2,256,256]{3,2,1,0:T(8,128)} %gates_hbm.1), custom_call_target="tpu_custom_call" | custom-call | flops 4294967296 | bytes 3145728 | tf_op jit(solution)/shard_map/section_operator/pallas_call | solution.py:200
  27.3 20.9 %all-to-all-done = f32[16,64,128]{2,1,0:T(8,128)S(1)} async-done(((f32[16,64,128]{2,1,0:T(8,128)}), f32[16,64,128]{2,1,0:T(8,128)S(1)}, u32[]{:S(2)}, u32[]{:S(2)}) %all-to-all-start) | async-done | bytes 524320 | tf_op jit(solution)/shard_map/all_to_all | solution.py:233
  48.2 1.8 %middle_section.1 = f32[64,2,8,128]{3,2,1,0:T(8,128)} custom-call(bf16[2048,512]{1,0:T(8,128)(2,1)S(1)} %section_operator.3.stack, f32[16,2,32,128]{3,2,1,0:T(8,128)S(1)} %bitcast.14), custom_call_target="tpu_custom_call" | custom-call | flops 805306368 | bytes 3145728 | tf_op jit(solution)/shard_map/middle_section/pallas_call | solution.py:221
  50.0 19.6 %all-to-all-start.1 = ((f32[64,16,128]{2,1,0:T(8,128)}), f32[64,16,128]{2,1,0:T(8,128)S(1)}, u32[]{:S(2)}, u32[]{:S(2)}) async-start(f32[64,16,128]{2,1,0:T(8,128)} %bitcast.5), calls=%async_computation.1 | async-start | bytes 1048576 | tf_op jit(solution)/shard_map/all_to_all | solution.py:233
  69.6 5.9 %section_operator.2.stack = bf16[2048,512]{1,0:T(8,128)(2,1)S(1)} custom-call(s32[6,8]{1,0:T(8,128)} %bits.5, s32[10]{0:T(128)} %plan.5, f32[6,2,256,256]{3,2,1,0:T(8,128)} %gates_hbm.1), custom_call_target="tpu_custom_call" | custom-call | flops 4294967296 | bytes 3145728 | tf_op jit(solution)/shard_map/section_operator/pallas_call | solution.py:200
  75.5 32.9 %all-to-all-done.1 = f32[64,16,128]{2,1,0:T(8,128)S(1)} async-done(((f32[64,16,128]{2,1,0:T(8,128)}), f32[64,16,128]{2,1,0:T(8,128)S(1)}, u32[]{:S(2)}, u32[]{:S(2)}) %all-to-all-start.1) | async-done | bytes 524320 | tf_op jit(solution)/shard_map/all_to_all | solution.py:233
  108.3 1.8 %last_section.1 = f32[1024,128]{1,0:T(8,128)} custom-call(bf16[2048,512]{1,0:T(8,128)(2,1)S(1)} %section_operator.2.stack, f32[64,2,8,128]{3,2,1,0:T(8,128)S(1)} %bitcast.15), custom_call_target="tpu_custom_call" | custom-call | flops 805306368 | bytes 3145728 | tf_op jit(solution)/shard_map/last_section/pallas_call | solution.py:221
Async XLA Ops:
  5.5 42.7 %all-to-all-start = ((f32[16,64,128]{2,1,0:T(8,128)}), f32[16,64,128]{2,1,0:T(8,128)S(1)}, u32[]{:S(2)}, u32[]{:S(2)}) async-start(f32[16,64,128]{2,1,0:T(8,128)} %bitcast.3), calls=%async_computation | async-start | bytes 1048576 | tf_op jit(solution)/shard_map/all_to_all | solution.py:233
  50.0 58.3 %all-to-all-start.1 = ((f32[64,16,128]{2,1,0:T(8,128)}), f32[64,16,128]{2,1,0:T(8,128)S(1)}, u32[]{:S(2)}, u32[]{:S(2)}) async-start(f32[64,16,128]{2,1,0:T(8,128)} %bitcast.5), calls=%async_computation.1 | async-start | bytes 1048576 | tf_op jit(solution)/shard_map/all_to_all | solution.py:233

commit v2 on v0

--- a/solution.py
+++ b/solution.py
@@ -173,7 +173,7 @@
     return pl.pallas_call(
         functools.partial(first_kernel, narrow_bits),
         grid=(1,),
-        out_shape=jax.ShapeDtypeStruct(shape, F32),
+        out_shape=vmem_shape(shape, F32),
         in_specs=[SMEM, SMEM, VMEM, gates_spec(0)],
         out_specs=VMEM,
         scratch_shapes=SCALARS,
@@ -186,7 +186,7 @@
     return pl.pallas_call(
         functools.partial(operator_kernel, section, order_in, order_out),
         grid=(1,),
-        out_shape=jax.ShapeDtypeStruct((4 * ROWS, ROWS), BF16),
+        out_shape=vmem_shape((4 * ROWS, ROWS), BF16),
         in_specs=[SMEM, SMEM, gates_spec(section)],
         out_specs=VMEM,
         scratch_shapes=SCALARS,
@@ -195,15 +195,23 @@
     )(bits, plan, gates)
 
 
-def run_section(kernel, stack, x, shape, name):
+def vmem_shape(shape, dtype):
+    return pltpu.VMEM(shape, dtype)
+
+
+def in_vmem(x):
+    return pltpu.with_memory_space_constraint(x, pltpu.VMEM)
+
+
+def run_section(kernel, stack, x, out_shape, name):
     return pl.pallas_call(
         kernel,
-        out_shape=jax.ShapeDtypeStruct(shape, F32),
+        out_shape=out_shape,
         in_specs=[VMEM, VMEM],
         out_specs=VMEM,
         cost_estimate=cost(24, 3 * 2**20),
         name=name,
-    )(stack, x)
+    )(in_vmem(stack), in_vmem(x))
 
 
 def exchange(blocks, axis):
@@ -231,11 +239,11 @@
     third = section_operator(2, gates, gate_bits, slot_plan, wide_order, natural)
     blocks = exchange(blocks, "narrow")
     wide = 2**wide_bits
-    blocks = run_section(
-        middle_kernel, second, blocks, (wide, 2, ROWS // wide, LANES), "middle_section"
-    )
+    shape = vmem_shape((wide, 2, ROWS // wide, LANES), F32)
+    blocks = run_section(middle_kernel, second, blocks, shape, "middle_section")
     blocks = exchange(blocks, "wide")
-    x = run_section(last_kernel, third, blocks, (2 * ROWS, LANES), "last_section")
+    shape = jax.ShapeDtypeStruct((2 * ROWS, LANES), F32)
+    x = run_section(last_kernel, third, blocks, shape, "last_section")
     return x.reshape(ROWS, 2, LANES).transpose(1, 0, 2).reshape(2, ROWS * LANES)
 
 

time: 115 us -> 110 us (0.957)
  Pallas kernels: 26.2 us -> 20.1 us
  waiting for transfers between devices: 51.1 us -> 53.7 us
  local copies, waits for them, and re-layouts: 1.58 us -> 0 us
    pallas_call x2, Pallas kernels: 6.91 us -> 3.57 us  [run_section(): pl.pallas_call(kernel, out_shape=out_shape, in_specs=[VMEM, VMEM], out_sp...]
    pallas_call x2, Pallas kernels: 14.5 us -> 11.8 us  [section_operator(): pl.pallas_call(functools.partial(operator_kernel, section, order_in, orde...]
    all_to_all x2, waiting for transfers between devices: 51.1 us -> 53.7 us  [exchange(): flat = lax.all_to_all(flat, axis, split_axis=0, concat_axis=0, tiled=True)]
    unnamed x4 -> x0, local copies, waits for them, and re-layouts: 1.58 us -> none
  transfers between devices with their start and end apart: 2 -> 2, of which waited for: 2 -> 2; matrix products, arithmetic and copies ran while one was open for 0% -> 0% of each run, Pallas kernels for 13% -> 11%
where the time goes in v2:
time: 110 us; the launch traced here: 109 us
  waiting for transfers between devices  53.7 us (49%)
  starting transfers between devices  35.5 us (32%)
  Pallas kernels  20.1 us (18%)
    all_to_all x2, waiting for transfers between devices, exchange(): flat = lax.all_to_all(flat, axis, split_axis=0, concat_axis=0, tiled=True)  53.7 us
    all_to_all x2, starting transfers between devices, exchange(): flat = lax.all_to_all(flat, axis, split_axis=0, concat_axis=0, tiled=True)  35.5 us
    pallas_call x2, Pallas kernels, section_operator(): pl.pallas_call(functools.partial(operator_kernel, section, order_in, orde...  11.8 us
    pallas_call x1, Pallas kernels, first_section(): pl.pallas_call(functools.partial(first_kernel, narrow_bits), grid=(1,), o...  4.76 us
    pallas_call x2, Pallas kernels, run_section(): pl.pallas_call(kernel, out_shape=out_shape, in_specs=[VMEM, VMEM], out_sp...  3.57 us
  transfers between devices with their start and end apart: 2, of which 2 were waited for; matrix products, arithmetic and copies ran while one was open for 0% of the time, Pallas kernels for 11%

profile of v2, /device:TPU:65, one launch (start us, length us, event | category | flops | bytes accessed | tf_op | source)
XLA Modules:
  0.0 109.4 jit_solution(16888109728394177206)
XLA Ops:
  0.0 4.8 %first_section.1 = f32[16,2,32,128]{3,2,1,0:T(8,128)} custom-call(s32[6,8]{1,0:T(8,128)} %bits.5, s32[10]{0:T(128)} %plan.5, f32[1024,128]{1,0:T(8,128)} %bitcast.16, f32[6,2,256,256]{3,2,1,0:T(8,128)} %gates.5), custom_call_target="tpu_custom_call" | custom-call | flops 1610612736 | bytes 2097152 | tf_op jit(solution)/shard_map/first_section/pallas_call | solution.py:173
  4.8 15.9 %all-to-all-start = ((f32[16,64,128]{2,1,0:T(8,128)}), f32[16,64,128]{2,1,0:T(8,128)S(1)}, u32[]{:S(2)}, u32[]{:S(2)}) async-start(f32[16,64,128]{2,1,0:T(8,128)} %bitcast.3), calls=%async_computation | async-start | bytes 1048576 | tf_op jit(solution)/shard_map/all_to_all | solution.py:219
  20.7 5.9 %section_operator.3.stack = bf16[2048,512]{1,0:T(8,128)(2,1)S(1)} custom-call(s32[6,8]{1,0:T(8,128)} %bits.5, s32[10]{0:T(128)} %plan.5, f32[6,2,256,256]{3,2,1,0:T(8,128)} %gates.5), custom_call_target="tpu_custom_call" | custom-call | flops 4294967296 | bytes 3145728 | tf_op jit(solution)/shard_map/section_operator/pallas_call | solution.py:186
  26.6 20.9 %all-to-all-done = f32[16,64,128]{2,1,0:T(8,128)S(1)} async-done(((f32[16,64,128]{2,1,0:T(8,128)}), f32[16,64,128]{2,1,0:T(8,128)S(1)}, u32[]{:S(2)}, u32[]{:S(2)}) %all-to-all-start) | async-done | bytes 524320 | tf_op jit(solution)/shard_map/all_to_all | solution.py:219
  47.5 1.8 %middle_section.1 = f32[64,2,8,128]{3,2,1,0:T(8,128)} custom-call(bf16[2048,512]{1,0:T(8,128)(2,1)S(1)} %section_operator.3.stack, f32[16,2,32,128]{3,2,1,0:T(8,128)S(1)} %bitcast.14), custom_call_target="tpu_custom_call" | custom-call | flops 805306368 | bytes 3145728 | tf_op jit(solution)/shard_map/middle_section/pallas_call | solution.py:207
  49.3 19.6 %all-to-all-start.1 = ((f32[64,16,128]{2,1,0:T(8,128)}), f32[64,16,128]{2,1,0:T(8,128)S(1)}, u32[]{:S(2)}, u32[]{:S(2)}) async-start(f32[64,16,128]{2,1,0:T(8,128)} %bitcast.5), calls=%async_computation.1 | async-start | bytes 1048576 | tf_op jit(solution)/shard_map/all_to_all | solution.py:219
  68.8 5.9 %section_operator.2.stack = bf16[2048,512]{1,0:T(8,128)(2,1)S(1)} custom-call(s32[6,8]{1,0:T(8,128)} %bits.5, s32[10]{0:T(128)} %plan.5, f32[6,2,256,256]{3,2,1,0:T(8,128)} %gates.5), custom_call_target="tpu_custom_call" | custom-call | flops 4294967296 | bytes 3145728 | tf_op jit(solution)/shard_map/section_operator/pallas_call | solution.py:186
  74.7 32.9 %all-to-all-done.1 = f32[64,16,128]{2,1,0:T(8,128)S(1)} async-done(((f32[64,16,128]{2,1,0:T(8,128)}), f32[64,16,128]{2,1,0:T(8,128)S(1)}, u32[]{:S(2)}, u32[]{:S(2)}) %all-to-all-start.1) | async-done | bytes 524320 | tf_op jit(solution)/shard_map/all_to_all | solution.py:219
  107.6 1.8 %last_section.1 = f32[1024,128]{1,0:T(8,128)} custom-call(bf16[2048,512]{1,0:T(8,128)(2,1)S(1)} %section_operator.2.stack, f32[64,2,8,128]{3,2,1,0:T(8,128)S(1)} %bitcast.15), custom_call_target="tpu_custom_call" | custom-call | flops 805306368 | bytes 3145728 | tf_op jit(solution)/shard_map/last_section/pallas_call | solution.py:207
Async XLA Ops:
  4.8 42.7 %all-to-all-start = ((f32[16,64,128]{2,1,0:T(8,128)}), f32[16,64,128]{2,1,0:T(8,128)S(1)}, u32[]{:S(2)}, u32[]{:S(2)}) async-start(f32[16,64,128]{2,1,0:T(8,128)} %bitcast.3), calls=%async_computation | async-start | bytes 1048576 | tf_op jit(solution)/shard_map/all_to_all | solution.py:219
  49.3 58.3 %all-to-all-start.1 = ((f32[64,16,128]{2,1,0:T(8,128)}), f32[64,16,128]{2,1,0:T(8,128)S(1)}, u32[]{:S(2)}, u32[]{:S(2)}) async-start(f32[64,16,128]{2,1,0:T(8,128)} %bitcast.5), calls=%async_computation.1 | async-start | bytes 1048576 | tf_op jit(solution)/shard_map/all_to_all | solution.py:219

commit v3 on v2

--- a/solution.py
+++ b/solution.py
@@ -34,8 +34,12 @@
     return used + [free]
 
 
-def plan_slots(plan, start, count, rest):
+def plan_slots(plan, start, count, rest, turned=None):
     slots = [plan[start + b] - LANE_BITS for b in range(count)]
+    if turned is not None:
+        half = count // 2
+        slots = [jnp.where(turned == 1, plan[start + (b + half) % count], plan[start + b]) for b in range(count)]
+        slots = [slot - LANE_BITS for slot in slots]
     filled = jnp.int32(0)
     for p in range(ROW_BITS):
         rest[filled] = jnp.int32(p)
@@ -106,11 +110,11 @@
     out[:, 1] = (parts[:, LANES : 2 * LANES] + parts[:, 3 * LANES :]).reshape(shape)
 
 
-def operator_kernel(section, order_in, order_out, bits, plan, gates, out, where, rest):
+def operator_kernel(section, order_in, order_out, bits, plan, core, gates, out, where, rest):
     order_a = gate_slots(bits, 2 * section)
     order_b = gate_slots(bits, 2 * section + 1)
-    columns = order_in(plan, rest)
-    result = order_out(plan, rest)
+    columns = order_in(plan, rest, core[0])
+    result = order_out(plan, rest, core[0])
     pick = permutation(columns, order_a, where)
     stack = stack_gate(gates[0, 0], gates[0, 1])
     picked = [mm(stack, pick[free * DIM : (free + 1) * DIM]).astype(BF16) for free in range(2)]
@@ -182,17 +186,17 @@
     )(bits, plan, x, gates)
 
 
-def section_operator(section, gates, bits, plan, order_in, order_out):
+def section_operator(section, gates, bits, plan, core, order_in, order_out):
     return pl.pallas_call(
         functools.partial(operator_kernel, section, order_in, order_out),
         grid=(1,),
         out_shape=vmem_shape((4 * ROWS, ROWS), BF16),
-        in_specs=[SMEM, SMEM, gates_spec(section)],
+        in_specs=[SMEM, SMEM, SMEM, gates_spec(section)],
         out_specs=VMEM,
         scratch_shapes=SCALARS,
         cost_estimate=cost(128, 3 * 2**20),
         name="section_operator",
-    )(bits, plan, gates)
+    )(bits, plan, core, gates)
 
 
 def vmem_shape(shape, dtype):
@@ -214,34 +218,68 @@
     )(in_vmem(stack), in_vmem(x))
 
 
-def exchange(blocks, axis):
+def exchange_narrow(blocks):
     flat = blocks.reshape(blocks.shape[0], -1, LANES)
-    flat = lax.all_to_all(flat, axis, split_axis=0, concat_axis=0, tiled=True)
+    flat = lax.all_to_all(flat, "narrow", split_axis=0, concat_axis=0, tiled=True)
     return flat.reshape(blocks.shape)
 
 
+def wide_groups(wide, narrow, high_on_even):
+    side = 2 ** ((wide.bit_length() - 1) // 2)
+    other = wide // side
+    groups = []
+    for n in range(narrow):
+        if (n % 2 == 0) == high_on_even:
+            groups += [[(j * side + k) * narrow + n for j in range(other)] for k in range(side)]
+        else:
+            groups += [[(k * side + j) * narrow + n for j in range(side)] for k in range(other)]
+    return groups
+
+
+def exchange_wide(blocks, wide, narrow):
+    side = 2 ** ((wide.bit_length() - 1) // 2)
+    square = blocks.reshape(side, side, -1, LANES)
+    for turn in range(2):
+        if turn:
+            square = square.transpose(1, 0, 2, 3)
+        square = lax.all_to_all(
+            square,
+            ("wide", "narrow"),
+            split_axis=0,
+            concat_axis=0,
+            tiled=True,
+            axis_index_groups=wide_groups(wide, narrow, turn == 0),
+        )
+    return square.reshape(blocks.shape)
+
+
 def shards(state, gates, gate_bits, slot_plan):
-    narrow_bits = lax.axis_size("narrow").bit_length() - 1
-    wide_bits = lax.axis_size("wide").bit_length() - 1
+    narrow = lax.axis_size("narrow")
+    wide = lax.axis_size("wide")
+    narrow_bits = narrow.bit_length() - 1
+    wide_bits = wide.bit_length() - 1
+    core = (lax.axis_index("narrow") % 2).astype(jnp.int32).reshape(1)
     x = state.reshape(2, ROWS, LANES).transpose(1, 0, 2).reshape(2 * ROWS, LANES)
 
-    def narrow_order(plan, rest):
+    def narrow_order(plan, rest, core):
         return plan_slots(plan, 0, narrow_bits, rest)
 
-    def wide_order(plan, rest):
-        return plan_slots(plan, narrow_bits, wide_bits, rest)
-
-    def natural(plan, rest):
+    def wide_order(plan, rest, core):
+        return plan_slots(plan, narrow_bits, wide_bits, rest, core)
+
+    def turned_order(plan, rest, core):
+        return plan_slots(plan, narrow_bits, wide_bits, rest, 1 - core)
+
+    def natural(plan, rest, core):
         return list(range(ROW_BITS))
 
     blocks = first_section(x, gates, gate_bits, slot_plan, narrow_bits)
-    second = section_operator(1, gates, gate_bits, slot_plan, narrow_order, wide_order)
-    third = section_operator(2, gates, gate_bits, slot_plan, wide_order, natural)
-    blocks = exchange(blocks, "narrow")
-    wide = 2**wide_bits
+    second = section_operator(1, gates, gate_bits, slot_plan, core, narrow_order, wide_order)
+    third = section_operator(2, gates, gate_bits, slot_plan, core, turned_order, natural)
+    blocks = exchange_narrow(blocks)
     shape = vmem_shape((wide, 2, ROWS // wide, LANES), F32)
     blocks = run_section(middle_kernel, second, blocks, shape, "middle_section")
-    blocks = exchange(blocks, "wide")
+    blocks = exchange_wide(blocks, wide, narrow)
     shape = jax.ShapeDtypeStruct((2 * ROWS, LANES), F32)
     x = run_section(last_kernel, third, blocks, shape, "last_section")
     return x.reshape(ROWS, 2, LANES).transpose(1, 0, 2).reshape(2, ROWS * LANES)

time: 110 us -> 108 us (0.982)
  blocking collectives: 0 us -> 37.2 us
  waiting for transfers between devices: 53.7 us -> 27.4 us
  starting transfers between devices: 35.5 us -> 22.9 us
    all_to_all x0 -> x1, blocking collectives: none -> 37.2 us  [exchange_wide(): lax.all_to_all(square, ('wide', 'narrow'), split_axis=0, concat_axis=0, t...]
    all_to_all x2, waiting for transfers between devices: 53.7 us -> 27.4 us  [the longest x1 20.9 us: exchange_narrow(): lax.all_to_all(flat, 'narrow', split_axis=0, concat_axis=0, tiled=True)]
    all_to_all x2, starting transfers between devices: 35.5 us -> 22.9 us  [the longest x1 15.9 us: exchange_narrow(): lax.all_to_all(flat, 'narrow', split_axis=0, concat_axis=0, tiled=True)]
where the time goes in v3:
time: 108 us
  blocking collectives  37.2 us (34%)
  waiting for transfers between devices  27.4 us (25%)
  starting transfers between devices  22.9 us (21%)
  Pallas kernels  19.3 us (18%)
    all_to_all x1, blocking collectives, exchange_wide(): lax.all_to_all(square, ('wide', 'narrow'), split_axis=0, concat_axis=0, t...  37.2 us
    all_to_all x1, waiting for transfers between devices, exchange_narrow(): lax.all_to_all(flat, 'narrow', split_axis=0, concat_axis=0, tiled=True)  20.9 us
    all_to_all x1, starting transfers between devices, exchange_narrow(): lax.all_to_all(flat, 'narrow', split_axis=0, concat_axis=0, tiled=True)  15.9 us
    pallas_call x2, Pallas kernels, section_operator(): pl.pallas_call(functools.partial(operator_kernel, section, order_in, orde...  11.8 us
    all_to_all x1, starting transfers between devices, exchange_wide(): lax.all_to_all(square, ('wide', 'narrow'), split_axis=0, concat_axis=0, t...  7.02 us
    all_to_all x1, waiting for transfers between devices, exchange_wide(): lax.all_to_all(square, ('wide', 'narrow'), split_axis=0, concat_axis=0, t...  6.51 us
    pallas_call x1, Pallas kernels, first_section(): pl.pallas_call(functools.partial(first_kernel, narrow_bits), grid=(1,), o...  4.76 us
    pallas_call x2, Pallas kernels, run_section(): pl.pallas_call(kernel, out_shape=out_shape, in_specs=[VMEM, VMEM], out_sp...  2.77 us
  transfers between devices with their start and end apart: 2, of which 2 were waited for; matrix products, arithmetic and copies ran while one was open for 0% of the time, Pallas kernels for 11%

profile of v3, /device:TPU:65, one launch (start us, length us, event | category | flops | bytes accessed | tf_op | source)
XLA Modules:
  0.0 107.7 jit_solution(7015397341107904168)
XLA Ops:
  0.0 4.8 %first_section.1 = f32[16,2,32,128]{3,2,1,0:T(8,128)} custom-call(s32[6,8]{1,0:T(8,128)} %bits.5, s32[10]{0:T(128)} %plan.5, f32[1024,128]{1,0:T(8,128)} %bitcast.20, f32[6,2,256,256]{3,2,1,0:T(8,128)} %gates.5), custom_call_target="tpu_custom_call" | custom-call | flops 1610612736 | bytes 2097152 | tf_op jit(solution)/shard_map/first_section/pallas_call | solution.py:177
  4.8 15.9 %all-to-all-start = ((f32[16,64,128]{2,1,0:T(8,128)}), f32[16,64,128]{2,1,0:T(8,128)S(1)}, u32[]{:S(2)}, u32[]{:S(2)}) async-start(f32[16,64,128]{2,1,0:T(8,128)} %bitcast.4), calls=%async_computation | async-start | bytes 1048576 | tf_op jit(solution)/shard_map/all_to_all | solution.py:223
  20.7 5.9 %section_operator.3.stack = bf16[2048,512]{1,0:T(8,128)(2,1)S(1)} custom-call(s32[6,8]{1,0:T(8,128)} %bits.5, s32[10]{0:T(128)} %plan.5, s32[1]{0:T(128)} %bitcast.core, f32[6,2,256,256]{3,2,1,0:T(8,128)} %gates.5), custom_call_target="tpu_custom_call" | custom-call | flops 4294967296 | bytes 3145728 | tf_op jit(solution)/shard_map/section_operator/pallas_call | solution.py:190
  26.6 20.9 %all-to-all-done = f32[16,64,128]{2,1,0:T(8,128)S(1)} async-done(((f32[16,64,128]{2,1,0:T(8,128)}), f32[16,64,128]{2,1,0:T(8,128)S(1)}, u32[]{:S(2)}, u32[]{:S(2)}) %all-to-all-start) | async-done | bytes 524320 | tf_op jit(solution)/shard_map/all_to_all | solution.py:223
  47.5 1.0 middle_section.1
  48.5 37.2 %all_to_all.15 = f32[8,8,16,128]{3,2,1,0:T(8,128)S(1)} all-to-all(f32[8,8,16,128]{3,2,1,0:T(8,128)S(1)} %bitcast.18), channel_id=1, replica_groups={{0,128,256,384,512,640,768,896},{16,144,272,400,528,656,784,912},{32,16..., dimensions={0} | all-to-all | bytes 1048576 | tf_op jit(solution)/shard_map/all_to_all | solution.py:245
  85.7 0.8 copy.12
  86.5 7.0 %all-to-all-start.2 = ((f32[8,8,16,128]{3,2,1,0:T(8,128)}), f32[8,8,16,128]{3,2,1,0:T(8,128)S(1)}, u32[]{:S(2)}, u32[]{:S(2)}) async-start(f32[8,8,16,128]{3,2,1,0:T(8,128)} %copy.12), calls=%async_computation.2 | async-start | bytes 1048576 | tf_op jit(solution)/shard_map/all_to_all | solution.py:245
  93.5 5.9 %section_operator.2.stack = bf16[2048,512]{1,0:T(8,128)(2,1)S(1)} custom-call(s32[6,8]{1,0:T(8,128)} %bits.5, s32[10]{0:T(128)} %plan.5, s32[1]{0:T(128)} %bitcast.core, f32[6,2,256,256]{3,2,1,0:T(8,128)} %gates.5), custom_call_target="tpu_custom_call" | custom-call | flops 4294967296 | bytes 3145728 | tf_op jit(solution)/shard_map/section_operator/pallas_call | solution.py:190
  99.4 6.5 %all-to-all-done.2 = f32[8,8,16,128]{3,2,1,0:T(8,128)S(1)} async-done(((f32[8,8,16,128]{3,2,1,0:T(8,128)}), f32[8,8,16,128]{3,2,1,0:T(8,128)S(1)}, u32[]{:S(2)}, u32[]{:S(2)}) %all-to-all-start.2) | async-done | bytes 524320 | tf_op jit(solution)/shard_map/all_to_all | solution.py:245
  105.9 1.8 %last_section.1 = f32[1024,128]{1,0:T(8,128)} custom-call(bf16[2048,512]{1,0:T(8,128)(2,1)S(1)} %section_operator.2.stack, f32[64,2,8,128]{3,2,1,0:T(8,128)S(1)} %bitcast.17), custom_call_target="tpu_custom_call" | custom-call | flops 805306368 | bytes 3145728 | tf_op jit(solution)/shard_map/last_section/pallas_call | solution.py:211
Async XLA Ops:
  4.8 42.7 %all-to-all-start = ((f32[16,64,128]{2,1,0:T(8,128)}), f32[16,64,128]{2,1,0:T(8,128)S(1)}, u32[]{:S(2)}, u32[]{:S(2)}) async-start(f32[16,64,128]{2,1,0:T(8,128)} %bitcast.4), calls=%async_computation | async-start | bytes 1048576 | tf_op jit(solution)/shard_map/all_to_all | solution.py:223
  86.5 19.4 %all-to-all-start.2 = ((f32[8,8,16,128]{3,2,1,0:T(8,128)}), f32[8,8,16,128]{3,2,1,0:T(8,128)S(1)}, u32[]{:S(2)}, u32[]{:S(2)}) async-start(f32[8,8,16,128]{3,2,1,0:T(8,128)} %copy.12), calls=%async_computation.2 | async-start | bytes 1048576 | tf_op jit(solution)/shard_map/all_to_all | solution.py:245

commit v4 on v3

--- a/solution.py
+++ b/solution.py
@@ -195,6 +195,7 @@
         out_specs=VMEM,
         scratch_shapes=SCALARS,
         cost_estimate=cost(128, 3 * 2**20),
+        compiler_params=pltpu.CompilerParams(vmem_limit_bytes=40 * 2**20),
         name="section_operator",
     )(bits, plan, core, gates)
 
@@ -276,6 +277,7 @@
     blocks = first_section(x, gates, gate_bits, slot_plan, narrow_bits)
     second = section_operator(1, gates, gate_bits, slot_plan, core, narrow_order, wide_order)
     third = section_operator(2, gates, gate_bits, slot_plan, core, turned_order, natural)
+    second, third = lax.optimization_barrier((second, third))
     blocks = exchange_narrow(blocks)
     shape = vmem_shape((wide, 2, ROWS // wide, LANES), F32)
     blocks = run_section(middle_kernel, second, blocks, shape, "middle_section")

time: 108 us -> 107 us (level)
  blocking collectives: 37.2 us -> 56.6 us
  waiting for transfers between devices: 27.4 us -> 13 us
  starting transfers between devices: 22.9 us -> 15.9 us
  local copies, waits for them, and re-layouts: 0.84 us -> 3.28 us
  Pallas kernels: 19.3 us -> 18.1 us
    all_to_all x1 -> x2, blocking collectives: 37.2 us -> 56.6 us  [exchange_wide(): lax.all_to_all(square, ('wide', 'narrow'), split_axis=0, concat_axis=0, t...]
    all_to_all x1, waiting for transfers between devices: 20.9 us -> 13 us  [exchange_narrow(): lax.all_to_all(flat, 'narrow', split_axis=0, concat_axis=0, tiled=True)]
    all_to_all x1 -> x0, starting transfers between devices: 7.02 us -> none  [exchange_wide(): lax.all_to_all(square, ('wide', 'narrow'), split_axis=0, concat_axis=0, t...]
    all_to_all x1 -> x0, waiting for transfers between devices: 6.51 us -> none  [exchange_wide(): lax.all_to_all(square, ('wide', 'narrow'), split_axis=0, concat_axis=0, t...]
    unnamed x0 -> x10, local copies, waits for them, and re-layouts: none -> 3.24 us
    pallas_call x2, Pallas kernels: 11.8 us -> 10.5 us  [section_operator(): pl.pallas_call(functools.partial(operator_kernel, section, order_in, orde...]
  transfers between devices with their start and end apart: 2 -> 1, of which waited for: 2 -> 1; matrix products, arithmetic and copies ran while one was open for 0% -> 0% of each run, Pallas kernels for 11% -> 10%
where the time goes in v4:
time: 107 us
  blocking collectives  56.6 us (53%)
  Pallas kernels  18.1 us (17%)
  starting transfers between devices  15.9 us (15%)
  waiting for transfers between devices  13 us (12%)
  local copies, waits for them, and re-layouts  3.28 us (3%)
    all_to_all x2, blocking collectives, exchange_wide(): lax.all_to_all(square, ('wide', 'narrow'), split_axis=0, concat_axis=0, t...  56.6 us
    all_to_all x1, starting transfers between devices, exchange_narrow(): lax.all_to_all(flat, 'narrow', split_axis=0, concat_axis=0, tiled=True)  15.9 us
    all_to_all x1, waiting for transfers between devices, exchange_narrow(): lax.all_to_all(flat, 'narrow', split_axis=0, concat_axis=0, tiled=True)  13 us
    pallas_call x2, Pallas kernels, section_operator(): pl.pallas_call(functools.partial(operator_kernel, section, order_in, orde...  10.5 us
    pallas_call x1, Pallas kernels, first_section(): pl.pallas_call(functools.partial(first_kernel, narrow_bits), grid=(1,), o...  4.78 us
    unnamed x10, local copies, waits for them, and re-layouts  3.24 us
    pallas_call x2, Pallas kernels, run_section(): pl.pallas_call(kernel, out_shape=out_shape, in_specs=[VMEM, VMEM], out_sp...  2.77 us
  transfers between devices with their start and end apart: 1, of which 1 were waited for; matrix products, arithmetic and copies ran while one was open for 0% of the time, Pallas kernels for 10%

profile of v4, /device:TPU:65, one launch (start us, length us, event | category | flops | bytes accessed | tf_op | source)
XLA Modules:
  0.0 107.0 jit_solution(9025194189327607829)
XLA Ops:
  0.0 0.0 copy-start.3
  0.0 0.0 copy-start.4
  0.0 4.8 %first_section.1 = f32[16,2,32,128]{3,2,1,0:T(8,128)} custom-call(s32[6,8]{1,0:T(8,128)} %bits.5, s32[10]{0:T(128)} %plan.5, f32[1024,128]{1,0:T(8,128)} %bitcast.20, f32[6,2,256,256]{3,2,1,0:T(8,128)} %gates.5), custom_call_target="tpu_custom_call" | custom-call | flops 1610612736 | bytes 2097152 | tf_op jit(solution)/shard_map/first_section/pallas_call | solution.py:177
  4.8 15.9 %all-to-all-start = ((f32[16,64,128]{2,1,0:T(8,128)}), f32[16,64,128]{2,1,0:T(8,128)S(1)}, u32[]{:S(2)}, u32[]{:S(2)}) async-start(f32[16,64,128]{2,1,0:T(8,128)} %bitcast.4), calls=%async_computation | async-start | bytes 1048576 | tf_op jit(solution)/shard_map/all_to_all | solution.py:224
  20.7 0.0 copy-done.3
  20.7 0.0 copy-done.4
  20.7 0.0 copy-start.2
  20.7 1.9 %copy-done.2 = f32[6,2,256,256]{3,2,1,0:T(8,128)S(1)} copy-done((f32[6,2,256,256]{3,2,1,0:T(8,128)S(1)}, f32[6,2,256,256]{3,2,1,0:T(8,128)}, u32[]{:S(2)}) %copy-start.2) | copy-done | bytes 3145752
  22.6 5.3 %section_operator.2.stack = bf16[2048,512]{1,0:T(8,128)(2,1)S(1)} custom-call(s32[6,8]{1,0:T(8,128)S(1)} %copy-done.3, s32[10]{0:T(128)S(1)} %copy-done.4, s32[1]{0:T(128)} %bitcast.core, f32[6,2,256,256]{3,2,1,0:T(8,128)S(1)} %copy-done.2), custom_call_target="tpu_custom_call" | custom-call | flops 4294967296 | bytes 3145728 | tf_op jit(solution)/shard_map/section_operator/pallas_call | solution.py:190
  27.9 5.3 %section_operator.3.stack = bf16[2048,512]{1,0:T(8,128)(2,1)S(1)} custom-call(s32[6,8]{1,0:T(8,128)S(1)} %copy-done.3, s32[10]{0:T(128)S(1)} %copy-done.4, s32[1]{0:T(128)} %bitcast.core, f32[6,2,256,256]{3,2,1,0:T(8,128)S(1)} %copy-done.2), custom_call_target="tpu_custom_call" | custom-call | flops 4294967296 | bytes 3145728 | tf_op jit(solution)/shard_map/section_operator/pallas_call | solution.py:190
  33.2 0.0 copy-start
  33.2 1.3 %copy-done = bf16[2048,512]{1,0:T(8,128)(2,1)} copy-done((bf16[2048,512]{1,0:T(8,128)(2,1)}, bf16[2048,512]{1,0:T(8,128)(2,1)S(1)}, u32[]{:S(2)}) %copy-start) | copy-done | bytes 2097176
  34.5 13.0 %all-to-all-done = f32[16,64,128]{2,1,0:T(8,128)S(1)} async-done(((f32[16,64,128]{2,1,0:T(8,128)}), f32[16,64,128]{2,1,0:T(8,128)S(1)}, u32[]{:S(2)}, u32[]{:S(2)}) %all-to-all-start) | async-done | bytes 524320 | tf_op jit(solution)/shard_map/all_to_all | solution.py:224
  47.5 1.0 middle_section.1
  48.5 0.0 copy-start.1
  48.5 37.4 %all_to_all.15 = f32[8,8,16,128]{3,2,1,0:T(8,128)S(1)} all-to-all(f32[8,8,16,128]{3,2,1,0:T(8,128)S(1)} %bitcast.17), channel_id=1, replica_groups={{0,128,256,384,512,640,768,896},{16,144,272,400,528,656,784,912},{32,16..., dimensions={0} | all-to-all | bytes 1048576 | tf_op jit(solution)/shard_map/all_to_all | solution.py:246
  86.0 19.2 %all_to_all.16 = f32[8,8,16,128]{3,2,1,0:T(8,128)S(1)} all-to-all(f32[8,8,16,128]{3,2,1,0:T(8,128)S(1)} %copy.12), channel_id=1, replica_groups={{0,16,32,48,64,80,96,112},{128,144,160,176,192,208,224,240},{256,272,28..., dimensions={0} | all-to-all | bytes 1048576 | tf_op jit(solution)/shard_map/all_to_all | solution.py:246
  105.2 0.0 copy-done.1
  105.2 1.8 %last_section.1 = f32[1024,128]{1,0:T(8,128)} custom-call(bf16[2048,512]{1,0:T(8,128)(2,1)S(1)} %copy-done.1, f32[64,2,8,128]{3,2,1,0:T(8,128)S(1)} %bitcast.18), custom_call_target="tpu_custom_call" | custom-call | flops 805306368 | bytes 3145728 | tf_op jit(solution)/shard_map/last_section/pallas_call | solution.py:212
  (1 shorter events, 0.0 us)
Async XLA Ops:
  0.0 20.7 %copy-start.3 = (s32[6,8]{1,0:T(8,128)S(1)}, s32[6,8]{1,0:T(8,128)}, u32[]{:S(2)}) copy-start(s32[6,8]{1,0:T(8,128)} %bits.5) | copy-start | bytes 580
  0.0 20.7 %copy-start.4 = (s32[10]{0:T(128)S(1)}, s32[10]{0:T(128)}, u32[]{:S(2)}) copy-start(s32[10]{0:T(128)} %plan.5) | copy-start | bytes 124
  4.8 42.7 %all-to-all-start = ((f32[16,64,128]{2,1,0:T(8,128)}), f32[16,64,128]{2,1,0:T(8,128)S(1)}, u32[]{:S(2)}, u32[]{:S(2)}) async-start(f32[16,64,128]{2,1,0:T(8,128)} %bitcast.4), calls=%async_computation | async-start | bytes 1048576 | tf_op jit(solution)/shard_map/all_to_all | solution.py:224
  20.7 1.9 %copy-start.2 = (f32[6,2,256,256]{3,2,1,0:T(8,128)S(1)}, f32[6,2,256,256]{3,2,1,0:T(8,128)}, u32[]{:S(2)}) copy-start(f32[6,2,256,256]{3,2,1,0:T(8,128)} %gates.5) | copy-start | bytes 9437188
  33.2 1.4 %copy-start = (bf16[2048,512]{1,0:T(8,128)(2,1)}, bf16[2048,512]{1,0:T(8,128)(2,1)S(1)}, u32[]{:S(2)}) copy-start(bf16[2048,512]{1,0:T(8,128)(2,1)S(1)} %section_operator.3.stack) | copy-start | bytes 6291460
  48.5 56.7 %copy-start.1 = (bf16[2048,512]{1,0:T(8,128)(2,1)S(1)}, bf16[2048,512]{1,0:T(8,128)(2,1)}, u32[]{:S(2)}) copy-start(bf16[2048,512]{1,0:T(8,128)(2,1)} %copy-done) | copy-start | bytes 6291460

commit v5 on v4

--- a/solution.py
+++ b/solution.py
@@ -143,22 +143,36 @@
     return complex_product(stack, high, low, LANES)
 
 
+def half_section(stack, x, part):
+    rows = stack[...].reshape(4, ROWS, ROWS)[:, part * DIM : (part + 1) * DIM]
+    return apply_section(rows.reshape(4 * DIM, ROWS), x[...])
+
+
 def middle_kernel(stack, x, out):
-    real, imag = apply_section(stack[...], x[...])
-    blocks = out.shape[0]
-    shape = (blocks, ROWS // blocks, LANES)
-    out[:, 0] = real.reshape(shape)
-    out[:, 1] = imag.reshape(shape)
-
-
-def last_kernel(stack, x, out):
-    real, imag = apply_section(stack[...], x[...])
-    out[pl.ds(0, ROWS, stride=2), :] = real
-    out[pl.ds(1, ROWS, stride=2), :] = imag
+    blocks = out.shape[0] // 2
+    shape = (blocks, DIM // blocks, LANES)
+    for part in range(2):
+        real, imag = half_section(stack, x, part)
+        out[part * blocks : (part + 1) * blocks, 0] = real.reshape(shape)
+        out[part * blocks : (part + 1) * blocks, 1] = imag.reshape(shape)
+
+
+def last_kernel(stack, x, out, held, sems):
+    copies = []
+    for part in range(2):
+        real, imag = half_section(stack, x, part)
+        held[part, pl.ds(0, DIM, stride=2), :] = real
+        held[part, pl.ds(1, DIM, stride=2), :] = imag
+        target = out.at[pl.ds(part * ROWS, ROWS)]
+        copies.append(pltpu.make_async_copy(held.at[part], target, sems.at[part]))
+        copies[-1].start()
+    for copy in copies:
+        copy.wait()
 
 
 SMEM = pl.BlockSpec(memory_space=pltpu.SMEM)
 VMEM = pl.BlockSpec(memory_space=pltpu.VMEM)
+ANY = pl.BlockSpec(memory_space=pl.ANY)
 SCALARS = [pltpu.SMEM((ROW_BITS,), jnp.int32), pltpu.SMEM((ROW_BITS + 1,), jnp.int32)]
 UNIT = 2 * DIM**3
 
@@ -208,12 +222,13 @@
     return pltpu.with_memory_space_constraint(x, pltpu.VMEM)
 
 
-def run_section(kernel, stack, x, out_shape, name):
+def run_section(kernel, stack, x, out_shape, name, out_specs=None, scratch_shapes=()):
     return pl.pallas_call(
         kernel,
         out_shape=out_shape,
         in_specs=[VMEM, VMEM],
-        out_specs=VMEM,
+        out_specs=VMEM if out_specs is None else out_specs,
+        scratch_shapes=scratch_shapes,
         cost_estimate=cost(24, 3 * 2**20),
         name=name,
     )(in_vmem(stack), in_vmem(x))
@@ -283,7 +298,8 @@
     blocks = run_section(middle_kernel, second, blocks, shape, "middle_section")
     blocks = exchange_wide(blocks, wide, narrow)
     shape = jax.ShapeDtypeStruct((2 * ROWS, LANES), F32)
-    x = run_section(last_kernel, third, blocks, shape, "last_section")
+    held = [pltpu.VMEM((2, ROWS, LANES), F32), pltpu.SemaphoreType.DMA((2,))]
+    x = run_section(last_kernel, third, blocks, shape, "last_section", ANY, held)
     return x.reshape(ROWS, 2, LANES).transpose(1, 0, 2).reshape(2, ROWS * LANES)
 
 

time: 107 us -> 107 us (level)
  no operation moved by 1% of the time
where the time goes in v5:
time: 107 us
  blocking collectives  56.6 us (53%)
  Pallas kernels  18.1 us (17%)
  starting transfers between devices  15.9 us (15%)
  waiting for transfers between devices  13 us (12%)
  local copies, waits for them, and re-layouts  3.28 us (3%)
    all_to_all x2, blocking collectives, exchange_wide(): lax.all_to_all(square, ('wide', 'narrow'), split_axis=0, concat_axis=0, t...  56.6 us
    all_to_all x1, starting transfers between devices, exchange_narrow(): lax.all_to_all(flat, 'narrow', split_axis=0, concat_axis=0, tiled=True)  15.9 us
    all_to_all x1, waiting for transfers between devices, exchange_narrow(): lax.all_to_all(flat, 'narrow', split_axis=0, concat_axis=0, tiled=True)  13 us
    pallas_call x2, Pallas kernels, section_operator(): pl.pallas_call(functools.partial(operator_kernel, section, order_in, orde...  10.5 us
    pallas_call x1, Pallas kernels, first_section(): pl.pallas_call(functools.partial(first_kernel, narrow_bits), grid=(1,), o...  4.78 us
    unnamed x10, local copies, waits for them, and re-layouts  3.24 us
    pallas_call x2, Pallas kernels, run_section(): pl.pallas_call(kernel, out_shape=out_shape, in_specs=[VMEM, VMEM], out_sp...  2.75 us
  transfers between devices with their start and end apart: 1, of which 1 were waited for; matrix products, arithmetic and copies ran while one was open for 0% of the time, Pallas kernels for 10%

profile of v5, /device:TPU:65, one launch (start us, length us, event | category | flops | bytes accessed | tf_op | source)
XLA Modules:
  0.0 106.9 jit_solution(17112399288008749696)
XLA Ops:
  0.0 0.0 copy-start.3
  0.0 0.0 copy-start.4
  0.0 4.8 %first_section.1 = f32[16,2,32,128]{3,2,1,0:T(8,128)} custom-call(s32[6,8]{1,0:T(8,128)} %bits.5, s32[10]{0:T(128)} %plan.5, f32[1024,128]{1,0:T(8,128)} %bitcast.20, f32[6,2,256,256]{3,2,1,0:T(8,128)} %gates.5), custom_call_target="tpu_custom_call" | custom-call | flops 1610612736 | bytes 2097152 | tf_op jit(solution)/shard_map/first_section/pallas_call | solution.py:191
  4.8 15.9 %all-to-all-start = ((f32[16,64,128]{2,1,0:T(8,128)}), f32[16,64,128]{2,1,0:T(8,128)S(1)}, u32[]{:S(2)}, u32[]{:S(2)}) async-start(f32[16,64,128]{2,1,0:T(8,128)} %bitcast.4), calls=%async_computation | async-start | bytes 1048576 | tf_op jit(solution)/shard_map/all_to_all | solution.py:239
  20.7 0.0 copy-done.3
  20.7 0.0 copy-done.4
  20.7 0.0 copy-start.2
  20.7 1.9 %copy-done.2 = f32[6,2,256,256]{3,2,1,0:T(8,128)S(1)} copy-done((f32[6,2,256,256]{3,2,1,0:T(8,128)S(1)}, f32[6,2,256,256]{3,2,1,0:T(8,128)}, u32[]{:S(2)}) %copy-start.2) | copy-done | bytes 3145752
  22.6 5.3 %section_operator.2.stack = bf16[2048,512]{1,0:T(8,128)(2,1)S(1)} custom-call(s32[6,8]{1,0:T(8,128)S(1)} %copy-done.3, s32[10]{0:T(128)S(1)} %copy-done.4, s32[1]{0:T(128)} %bitcast.core, f32[6,2,256,256]{3,2,1,0:T(8,128)S(1)} %copy-done.2), custom_call_target="tpu_custom_call" | custom-call | flops 4294967296 | bytes 3145728 | tf_op jit(solution)/shard_map/section_operator/pallas_call | solution.py:204
  27.9 5.3 %section_operator.3.stack = bf16[2048,512]{1,0:T(8,128)(2,1)S(1)} custom-call(s32[6,8]{1,0:T(8,128)S(1)} %copy-done.3, s32[10]{0:T(128)S(1)} %copy-done.4, s32[1]{0:T(128)} %bitcast.core, f32[6,2,256,256]{3,2,1,0:T(8,128)S(1)} %copy-done.2), custom_call_target="tpu_custom_call" | custom-call | flops 4294967296 | bytes 3145728 | tf_op jit(solution)/shard_map/section_operator/pallas_call | solution.py:204
  33.2 0.0 copy-start
  33.2 1.3 %copy-done = bf16[2048,512]{1,0:T(8,128)(2,1)} copy-done((bf16[2048,512]{1,0:T(8,128)(2,1)}, bf16[2048,512]{1,0:T(8,128)(2,1)S(1)}, u32[]{:S(2)}) %copy-start) | copy-done | bytes 2097176
  34.5 13.0 %all-to-all-done = f32[16,64,128]{2,1,0:T(8,128)S(1)} async-done(((f32[16,64,128]{2,1,0:T(8,128)}), f32[16,64,128]{2,1,0:T(8,128)S(1)}, u32[]{:S(2)}, u32[]{:S(2)}) %all-to-all-start) | async-done | bytes 524320 | tf_op jit(solution)/shard_map/all_to_all | solution.py:239
  47.5 1.0 middle_section.1
  48.5 0.0 copy-start.1
  48.5 37.4 %all_to_all.15 = f32[8,8,16,128]{3,2,1,0:T(8,128)S(1)} all-to-all(f32[8,8,16,128]{3,2,1,0:T(8,128)S(1)} %bitcast.17), channel_id=1, replica_groups={{0,128,256,384,512,640,768,896},{16,144,272,400,528,656,784,912},{32,16..., dimensions={0} | all-to-all | bytes 1048576 | tf_op jit(solution)/shard_map/all_to_all | solution.py:261
  86.0 19.2 %all_to_all.16 = f32[8,8,16,128]{3,2,1,0:T(8,128)S(1)} all-to-all(f32[8,8,16,128]{3,2,1,0:T(8,128)S(1)} %copy.12), channel_id=1, replica_groups={{0,16,32,48,64,80,96,112},{128,144,160,176,192,208,224,240},{256,272,28..., dimensions={0} | all-to-all | bytes 1048576 | tf_op jit(solution)/shard_map/all_to_all | solution.py:261
  105.2 0.0 copy-done.1
  105.2 1.8 %last_section.1 = f32[1024,128]{1,0:T(8,128)} custom-call(bf16[2048,512]{1,0:T(8,128)(2,1)S(1)} %copy-done.1, f32[64,2,8,128]{3,2,1,0:T(8,128)S(1)} %bitcast.18), custom_call_target="tpu_custom_call" | custom-call | flops 805306368 | bytes 3145728 | tf_op jit(solution)/shard_map/last_section/pallas_call | solution.py:226
  (1 shorter events, 0.0 us)
Async XLA Ops:
  0.0 20.7 %copy-start.3 = (s32[6,8]{1,0:T(8,128)S(1)}, s32[6,8]{1,0:T(8,128)}, u32[]{:S(2)}) copy-start(s32[6,8]{1,0:T(8,128)} %bits.5) | copy-start | bytes 580
  0.0 20.7 %copy-start.4 = (s32[10]{0:T(128)S(1)}, s32[10]{0:T(128)}, u32[]{:S(2)}) copy-start(s32[10]{0:T(128)} %plan.5) | copy-start | bytes 124
  4.8 42.7 %all-to-all-start = ((f32[16,64,128]{2,1,0:T(8,128)}), f32[16,64,128]{2,1,0:T(8,128)S(1)}, u32[]{:S(2)}, u32[]{:S(2)}) async-start(f32[16,64,128]{2,1,0:T(8,128)} %bitcast.4), calls=%async_computation | async-start | bytes 1048576 | tf_op jit(solution)/shard_map/all_to_all | solution.py:239
  20.7 1.9 %copy-start.2 = (f32[6,2,256,256]{3,2,1,0:T(8,128)S(1)}, f32[6,2,256,256]{3,2,1,0:T(8,128)}, u32[]{:S(2)}) copy-start(f32[6,2,256,256]{3,2,1,0:T(8,128)} %gates.5) | copy-start | bytes 9437188
  33.2 1.4 %copy-start = (bf16[2048,512]{1,0:T(8,128)(2,1)}, bf16[2048,512]{1,0:T(8,128)(2,1)S(1)}, u32[]{:S(2)}) copy-start(bf16[2048,512]{1,0:T(8,128)(2,1)S(1)} %section_operator.3.stack) | copy-start | bytes 6291460
  48.5 56.7 %copy-start.1 = (bf16[2048,512]{1,0:T(8,128)(2,1)S(1)}, bf16[2048,512]{1,0:T(8,128)(2,1)}, u32[]{:S(2)}) copy-start(bf16[2048,512]{1,0:T(8,128)(2,1)} %copy-done) | copy-start | bytes 6291460
